TPU v7x, 512 devices: a whole 4x4x16 slice. The times are simulated.
512 devices in a mesh: section: 8 (over y_hi, x), head: 4 (over y_lo, core), tok: 16 (over z).
Axes of the slice: x: 4, y: 4 (y_hi: 2, y_lo: 2; y = y_hi * 2 + y_lo), z: 16, core: 2. Of those that a mesh axis runs over, the one named last changes fastest.
Arguments:
- held_cotangents: bfloat16 [8, 2, 2048, 2560], P('section', None, 'tok', 'head'), may hold values from -6 to 6
- entering_adjoint: bfloat16 [2048, 2560], P('tok', 'head'), may hold values from -6 to 6
- saved_queries: bfloat16 [8, 2048, 2560], P('section', 'tok', 'head'), may hold values from -1024 to 1024
- saved_keys: bfloat16 [8, 2048, 2560], P('section', 'tok', 'head'), may hold values from -20 to 20
- value_weight: bfloat16 [8, 2560, 2560], P('section', None, 'head'), may hold values from -0.125 to 0.125
- out_weight: bfloat16 [8, 2560, 2560], P('section', 'tok', 'head'), may hold values from -0.125 to 0.125
- block_gate: float32 [8, 2560], P('section'), may hold values from -3 to 3
- time_gate: float32 [32, 2560], replicated, may hold values from -3 to 3
- timestep: int32 [1], replicated, may hold values from 0 to 31
Outputs:
- passed: bfloat16 [8, 2, 2048, 2560], P('section', None, 'tok', 'head')
All inputs are finite; a program needn't handle non-finite values.
Results may differ from a plain program's by a relative error of at most 0.0085.
Values may be sent and summed in bfloat16 or wider, within the bound.
A program may use at most 64 MiB of HBM per device.

v0:
```python
import jax
import jax.numpy as jnp
from jax import lax
from jax.sharding import PartitionSpec as P

HD = 128
GUIDE = 3.0


def shifted(value, axis, steps):
    count = lax.axis_size(axis)
    leading, last = (max(0, -steps), min(count, count - steps))
    return lax.ppermute(value, axis, [(source, source + steps) for source in range(leading, last)])


def shards(
    held_cotangents,
    entering_adjoint,
    saved_queries,
    saved_keys,
    value_weight,
    out_weight,
    block_gate,
    time_gate,
    timestep,
):
    steps_index = jnp.arange(time_gate.shape[0])
    time_row = jnp.sum(
        jnp.where((steps_index == timestep[0])[:, None], time_gate, jnp.zeros_like(time_gate)),
        axis=0,
    )
    gate_row = block_gate[0] + time_row
    whole_cot = lax.all_gather(held_cotangents[0], "head", axis=2, tiled=True)
    scaled = (whole_cot.astype(jnp.float32) * gate_row).astype(jnp.bfloat16)
    out_full = lax.all_gather(out_weight[0], "tok", axis=0, tiled=True)
    attn_grad = jnp.einsum(
        "btd,dk->btk", scaled, out_full, preferred_element_type=jnp.float32
    ).astype(jnp.bfloat16)
    rows_here = saved_queries.shape[1]
    groups_here = saved_queries.shape[2] // HD
    score_scale = HD ** (-0.5)
    normal_grad = attn_grad[0]
    key_all = lax.all_gather(saved_keys[0], "tok", axis=0, tiled=True)
    key_heads = key_all.reshape(key_all.shape[0], groups_here, HD)
    query_heads = saved_queries[0].reshape(rows_here, groups_here, HD)
    scores = (
        jnp.einsum("ihe,jhe->hij", query_heads, key_heads, preferred_element_type=jnp.float32)
        * score_scale
    )
    row_top = jnp.max(scores, axis=2, keepdims=True)
    log_total = row_top + jnp.log(jnp.sum(jnp.exp(scores - row_top), axis=2, keepdims=True))
    weights = jnp.exp(scores - log_total).astype(jnp.bfloat16)
    grad_heads = normal_grad.reshape(rows_here, groups_here, HD)
    terms = jnp.einsum("hij,ihe->jhe", weights, grad_heads, preferred_element_type=jnp.float32)
    value_grad = lax.psum_scatter(
        terms.reshape(lax.axis_size("tok") * rows_here, groups_here * HD).astype(jnp.bfloat16),
        "tok",
        scatter_dimension=0,
        tiled=True,
    )
    stacked = jnp.stack([value_grad, attn_grad[1]])
    partial_back = jnp.einsum(
        "btk,dk->btd", stacked, value_weight[0], preferred_element_type=jnp.float32
    )
    back_sum = lax.psum_scatter(
        partial_back.astype(jnp.bfloat16), "head", scatter_dimension=2, tiled=True
    ).astype(jnp.float32)
    block_cot = (held_cotangents[0].astype(jnp.float32) + back_sum).astype(jnp.bfloat16)
    passed_on = shifted(block_cot, "section", -1)
    entering_full = entering_adjoint.astype(jnp.float32)
    fresh_rows = jnp.stack([(1.0 + GUIDE) * entering_full, -GUIDE * entering_full]).astype(
        jnp.bfloat16
    )
    is_last = lax.axis_index("section") == lax.axis_size("section") - 1
    return jnp.where(is_last, fresh_rows, passed_on)[None]


def solution(mesh):
    return jax.shard_map(
        shards,
        mesh=mesh,
        in_specs=(
            P("section", None, "tok", "head"),
            P("tok", "head"),
            P("section", "tok", "head"),
            P("section", "tok", "head"),
            P("section", None, "head"),
            P("section", "tok", "head"),
            P("section", None),
            P(),
            P(),
        ),
        out_specs=P("section", None, "tok", "head"),
        check_vma=False,
    )
```

profile of v0, /device:TPU:6, one launch (start us, length us, event | category | flops | bytes accessed | tf_op | source)
XLA Modules:
  0.0 357.0 jit_solution(16926532515218221262)
XLA Ops:
  6.5 1.9 copy.21
  10.6 1.1 copy.20
  12.4 1.1 select_reduce_fusion
  13.5 83.0 %all-gather.11.cloned.1.call-done = bf16[1,2048,640]{1,2,0:T(8,128)(2,1)} async-done(((bf16[1,128,640]{1,2,0:T(8,128)(2,1)}), bf16[1,2048,640]{1,2,0:T(8,128)(2,1)}) %all-gather.11.cloned.1.call-update) | async-done | bytes 2621456 | tf_op jit(solution)/shard_map/all_gather | solution.py:43
  96.6 2.7 multiply_reduce_fusion
  99.3 2.3 copy-done.1
  101.6 1.0 exponential_reduce_fusion
  102.6 21.9 %all-gather.7.cloned.1.call-done = bf16[1,2,128,2560]{3,2,1,0:T(8,128)(2,1)} async-done(((bf16[1,2,128,640]{3,2,1,0:T(8,128)(2,1)}), bf16[1,2,128,2560]{3,2,1,0:T(8,128)(2,1)}) %all-gather.7.cloned.1.call-update) | async-done | bytes 1310736 | tf_op jit(solution)/shard_map/all_gather | solution.py:33
  124.5 79.6 %all-gather.9.cloned.1.call-done = bf16[1,2560,640]{2,1,0:T(8,128)(2,1)} async-done(((bf16[1,160,640]{2,1,0:T(8,128)(2,1)}), bf16[1,2560,640]{2,1,0:T(8,128)(2,1)}) %all-gather.9.cloned.1.call-update) | async-done | bytes 3276816 | tf_op jit(solution)/shard_map/all_gather | solution.py:35
  204.2 3.5 fusion.9
  208.4 0.8 copy.19
  209.2 5.3 %convolution_convert_fusion.1 = bf16[5,128,2048]{2,1,0:T(8,128)(2,1)} fusion(bf16[128,5,128]{0,2,1:T(8,128)(2,1)} %bitcast.51, f32[5,128,2048]{2,1,0:T(8,128)} %copy-done.1, f32[5,128]{1,0:T(8,128)S(1)} %log_add_fusion), kind=kOutput, calls=%fused_computation.7 | convolution fusion | flops 340787200 | bytes 8030720 | tf_op jit(solution)/shard_map/hij,ihe->jhe/dot_general | solution.py:54
  214.5 4.4 %copy.24 = bf16[2048,640]{1,0:T(8,128)(2,1)} copy(bf16[2048,640]{0,1:T(8,128)(2,1)} %bitcast.45) | data formatting | bytes 5242880 | tf_op jit(solution)/shard_map/convert_element_type | solution.py:56
  219.0 71.2 %reduce-scatter.5.cloned.1.call-done = bf16[128,640]{1,0:T(8,128)(2,1)} async-done(((bf16[2048,640]{1,0:T(8,128)(2,1)}), bf16[128,640]{1,0:T(8,128)(2,1)}) %reduce-scatter.5.cloned.1.call-update) | async-done | bytes 163856 | tf_op jit(solution)/shard_map/reduce_scatter | solution.py:55
  290.2 3.2 convolution_convert_fusion
  293.4 4.3 %copy.27 = bf16[2,128,2560]{1,0,2:T(2,128)(2,1)} copy(bf16[2,128,2560]{2,1,0:T(8,128)(2,1)} %convolution_convert_fusion) | data formatting | bytes 2621440
  297.7 2.6 copy.31
  300.3 27.3 %reduce-scatter.7.cloned.1.call-done = bf16[640,256]{1,0:T(8,128)(2,1)} async-done(((bf16[2560,256]{1,0:T(8,128)(2,1)}), bf16[640,256]{1,0:T(8,128)(2,1)}) %reduce-scatter.7.cloned.1.call-update) | async-done | bytes 327696
  327.6 1.8 reshape.35
  329.4 1.9 copy.28
  331.3 1.9 fusion.14
  333.2 2.7 collective-permute-start
  336.0 12.7 %collective-permute-done = bf16[2,128,640]{2,1,0:T(8,128)(2,1)} collective-permute-done((bf16[2,128,640]{2,1,0:T(8,128)(2,1)}, bf16[2,128,640]{2,1,0:T(8,128)(2,1)}, u32[]{:S(2)}, u32[]{:S(2)}) %collective-permute-start) | collective-permute-done | bytes 327712 | tf_op jit(solution)/shard_map/ppermute | solution.py:13
  348.8 1.7 fusion.17
  (23 shorter events, 3.1 us)
Async XLA Ops:
  6.5 283.7 %copy-start = (bf16[1,2560,640]{2,1,0:T(8,128)(2,1)S(1)}, bf16[1,2560,640]{2,1,0:T(8,128)(2,1)}, u32[]{:S(2)}) copy-start(bf16[1,2560,640]{2,1,0:T(8,128)(2,1)} %param.13) | copy-start | bytes 9830404
  6.5 90.0 %all-gather.11.cloned.1.call-start = ((), (), s32[]{:S(2)}) async-start(), calls=%async_computation.5 | async-start | bytes 2785280 | tf_op jit(solution)/shard_map/all_gather | solution.py:43
  8.4 116.1 %all-gather.7.cloned.1.call-start = ((), (), s32[]{:S(2)}) async-start(), calls=%async_computation.3 | async-start | bytes 1638400 | tf_op jit(solution)/shard_map/all_gather | solution.py:33
  9.2 195.0 %all-gather.9.cloned.1.call-start = ((), (), s32[]{:S(2)}) async-start(), calls=%async_computation.4 | async-start | bytes 3481600 | tf_op jit(solution)/shard_map/all_gather | solution.py:35
  9.9 280.3 %reduce-scatter.5.cloned.1.call-start = ((), (), s32[]{:S(2)}) async-start(), calls=%async_computation.2 | async-start | bytes 2785280 | tf_op jit(solution)/shard_map/reduce_scatter | solution.py:55
  99.3 2.3 copy-start.1
  214.5 75.7 %copy-start.2 = (bf16[1,128,640]{2,1,0:T(8,128)(2,1)S(1)}, bf16[1,128,640]{2,1,0:T(8,128)(2,1)}, u32[]{:S(2)}) copy-start(bf16[1,128,640]{2,1,0:T(8,128)(2,1)} %get-tuple-element.6) | copy-start | bytes 491524
  218.9 108.7 %reduce-scatter.7.cloned.1.call-start = ((), (), s32[]{:S(2)}) async-start(), calls=%async_computation.6 | async-start | bytes 1638400
  297.7 38.3 %copy-start.3 = (bf16[128,640]{1,0:T(8,128)(2,1)S(1)}, bf16[128,640]{1,0:T(8,128)(2,1)}, u32[]{:S(2)}) copy-start(bf16[128,640]{1,0:T(8,128)(2,1)} %param.10) | copy-start | bytes 491524
  333.2 15.6 %collective-permute-start = (bf16[2,128,640]{2,1,0:T(8,128)(2,1)}, bf16[2,128,640]{2,1,0:T(8,128)(2,1)}, u32[]{:S(2)}, u32[]{:S(2)}) collective-permute-start(bf16[2,128,640]{2,1,0:T(8,128)(2,1)} %fusion.14), channel_id=1, source_target_pairs={{64,0},{128,64},{192,128},{256,192},{320,256},{384,320},{448,384},... | collective-permute-start | bytes 983048 | tf_op jit(solution)/shard_map/ppermute | solution.py:13
Sparse Core Ops, SparseCore 0:
  9.4 87.1 all-gather.10
  98.7 25.7 all-gather.6
  126.6 77.5 all-gather.8
  219.1 71.0 reduce-scatter.4
  300.4 27.1 reduce-scatter.6
where the time goes:
time: 358 us; the launch traced here: 357 us
  waiting for transfers between devices  297 us (83%)
  local copies, waits for them, and re-layouts  21.7 us (6%)
  matrix products  14.7 us (4%)
  between operations  13.9 us (4%)
  other arithmetic  6.49 us (2%)
    all_gather x1, waiting for transfers between devices, shards(): key_all = lax.all_gather(saved_keys[0], 'tok', axis=0, tiled=True)  83 us
    all_gather x1, waiting for transfers between devices, shards(): out_full = lax.all_gather(out_weight[0], 'tok', axis=0, tiled=True)  79.6 us
    reduce_scatter x1, waiting for transfers between devices, shards(): lax.psum_scatter(terms.reshape(lax.axis_size('tok') * rows_here, groups_h...  71.2 us
    unnamed x6, waiting for transfers between devices  28.7 us
    all_gather x1, waiting for transfers between devices, shards(): whole_cot = lax.all_gather(held_cotangents[0], 'head', axis=2, tiled=True)  21.9 us
    unnamed x14, local copies, waits for them, and re-layouts  15.8 us
    ppermute x1, waiting for transfers between devices, shifted(): lax.ppermute(value, axis, [(source, source + steps) for source in range(l...  12.7 us
  transfers between devices with their start and end apart: 6, of which 6 were waited for; matrix products, arithmetic and copies ran while one was open for 2% of the time, Pallas kernels for 0%

commit v1 on v0

--- a/solution.py
+++ b/solution.py
@@ -5,6 +5,18 @@
 
 HD = 128
 GUIDE = 3.0
+
+
+def ring_product(shard, axis, dim, contribution):
+    size, index = (lax.axis_size(axis), lax.axis_index(axis))
+    behind = [(i, (i - 1) % size) for i in range(size)]
+    rows = shard.shape[dim]
+    carried = shard
+    total = contribution(carried, index * rows)
+    for step in range(1, size):
+        carried = lax.ppermute(carried, axis, behind)
+        total = total + contribution(carried, (index + step) % size * rows)
+    return total
 
 
 def shifted(value, axis, steps):
@@ -32,9 +44,16 @@
     gate_row = block_gate[0] + time_row
     whole_cot = lax.all_gather(held_cotangents[0], "head", axis=2, tiled=True)
     scaled = (whole_cot.astype(jnp.float32) * gate_row).astype(jnp.bfloat16)
-    out_full = lax.all_gather(out_weight[0], "tok", axis=0, tiled=True)
-    attn_grad = jnp.einsum(
-        "btd,dk->btk", scaled, out_full, preferred_element_type=jnp.float32
+    attn_grad = ring_product(
+        out_weight[0],
+        "tok",
+        0,
+        lambda own_block, at: jnp.einsum(
+            "btd,dk->btk",
+            lax.dynamic_slice_in_dim(scaled, at, own_block.shape[0], axis=2),
+            own_block,
+            preferred_element_type=jnp.float32,
+        ),
     ).astype(jnp.bfloat16)
     rows_here = saved_queries.shape[1]
     groups_here = saved_queries.shape[2] // HD

time: 358 us -> 327 us (0.913)
  waiting for transfers between devices: 297 us -> 170 us
  starting transfers between devices: 2.91 us -> 90.1 us
  local copies, waits for them, and re-layouts: 21.7 us -> 27 us
    ppermute x0 -> x15, starting transfers between devices: none -> 87.3 us  [ring_product(): carried = lax.ppermute(carried, axis, behind)]
    all_gather x1 -> x0, waiting for transfers between devices: 79.6 us -> none  [shards(): out_full = lax.all_gather(out_weight[0], 'tok', axis=0, tiled=True)]
    all_gather x1, waiting for transfers between devices: 83 us -> 8.76 us  [shards(): key_all = lax.all_gather(saved_keys[0], 'tok', axis=0, tiled=True)]
    ppermute x0 -> x15, waiting for transfers between devices: none -> 48.8 us  [ring_product(): carried = lax.ppermute(carried, axis, behind)]
    all_gather x1, waiting for transfers between devices: 21.9 us -> 0.02 us  [shards(): whole_cot = lax.all_gather(held_cotangents[0], 'head', axis=2, tiled=True)]
    unnamed x14 -> x47, local copies, waits for them, and re-layouts: 15.8 us -> 21.1 us
    dot_general x1 -> x16, matrix products: 3.51 us -> 7.67 us  [shards(): jnp.einsum('btd,dk->btk', lax.dynamic_slice_in_dim(scaled, at, own_block....]
    unnamed x6 -> x5, waiting for transfers between devices: 28.7 us -> 27.3 us
  transfers between devices with their start and end apart: 6 -> 20, of which waited for: 6 -> 18; matrix products, arithmetic and copies ran while one was open for 2% -> 5% of each run, Pallas kernels for 0% -> 0%
where the time goes in v1:
time: 327 us; the launch traced here: 326 us
  waiting for transfers between devices  170 us (52%)
  starting transfers between devices  90.1 us (28%)
  local copies, waits for them, and re-layouts  27 us (8%)
  matrix products  16.4 us (5%)
  between operations  14.5 us (4%)
  other arithmetic  7.54 us (2%)
    ppermute x15, starting transfers between devices, ring_product(): carried = lax.ppermute(carried, axis, behind)  87.3 us
    reduce_scatter x1, waiting for transfers between devices, shards(): lax.psum_scatter(terms.reshape(lax.axis_size('tok') * rows_here, groups_h...  72.6 us
    ppermute x15, waiting for transfers between devices, ring_product(): carried = lax.ppermute(carried, axis, behind)  48.8 us
    unnamed x5, waiting for transfers between devices  27.3 us
    unnamed x47, local copies, waits for them, and re-layouts  21.1 us
    ppermute x1, waiting for transfers between devices, shifted(): lax.ppermute(value, axis, [(source, source + steps) for source in range(l...  12.7 us
    all_gather x1, waiting for transfers between devices, shards(): key_all = lax.all_gather(saved_keys[0], 'tok', axis=0, tiled=True)  8.76 us
    dot_general x16, matrix products, shards(): jnp.einsum('btd,dk->btk', lax.dynamic_slice_in_dim(scaled, at, own_block....  7.67 us
  transfers between devices with their start and end apart: 20, of which 18 were waited for; matrix products, arithmetic and copies ran while one was open for 5% of the time, Pallas kernels for 0%

profile of v1, /device:TPU:6, one launch (start us, length us, event | category | flops | bytes accessed | tf_op | source)
XLA Modules:
  0.0 325.8 jit_solution(11323899774507397955)
XLA Ops:
  8.6 11.4 %collective-permute-start = (bf16[160,640]{1,0:T(8,128)(2,1)}, bf16[160,640]{1,0:T(8,128)(2,1)S(1)}, u32[]{:S(2)}, u32[]{:S(2)}) collective-permute-start(bf16[160,640]{1,0:T(8,128)(2,1)} %bitcast.90), channel_id=1, source_target_pairs={{0,15},{1,0},{2,1},{3,2},{4,3},{5,4},{6,5},{7,6},{8,7},{9,8},{10,9... | collective-permute-start | bytes 614408 | tf_op jit(solution)/shard_map/ppermute | solution.py:17
  20.1 4.6 %collective-permute-done = bf16[160,640]{1,0:T(8,128)(2,1)S(1)} collective-permute-done((bf16[160,640]{1,0:T(8,128)(2,1)}, bf16[160,640]{1,0:T(8,128)(2,1)S(1)}, u32[]{:S(2)}, u32[]{:S(2)}) %collective-permute-start) | collective-permute-done | bytes 204832 | tf_op jit(solution)/shard_map/ppermute | solution.py:17
  25.4 5.5 %collective-permute-start.1 = (bf16[160,640]{1,0:T(8,128)(2,1)S(1)}, bf16[160,640]{1,0:T(8,128)(2,1)S(1)}, u32[]{:S(2)}, u32[]{:S(2)}) collective-permute-start(bf16[160,640]{1,0:T(8,128)(2,1)S(1)} %collective-permute-done), channel_id=1, source_target_pairs={{0,15},{1,0},{2,1},{3,2},{4,3},{5,4},{6,5},{7,6},{8,7},{9,8},{10,9... | collective-permute-start | bytes 614408 | tf_op jit(solution)/shard_map/ppermute | solution.py:17
  35.0 5.6 %collective-permute-start.2 = (bf16[160,640]{1,0:T(8,128)(2,1)S(1)}, bf16[160,640]{1,0:T(8,128)(2,1)S(1)}, u32[]{:S(2)}, u32[]{:S(2)}) collective-permute-start(bf16[160,640]{1,0:T(8,128)(2,1)S(1)} %collective-permute-done.1), channel_id=1, source_target_pairs={{0,15},{1,0},{2,1},{3,2},{4,3},{5,4},{6,5},{7,6},{8,7},{9,8},{10,9... | collective-permute-start | bytes 614408 | tf_op jit(solution)/shard_map/ppermute | solution.py:17
  44.5 5.6 %collective-permute-start.3 = (bf16[160,640]{1,0:T(8,128)(2,1)S(1)}, bf16[160,640]{1,0:T(8,128)(2,1)S(1)}, u32[]{:S(2)}, u32[]{:S(2)}) collective-permute-start(bf16[160,640]{1,0:T(8,128)(2,1)S(1)} %collective-permute-done.2), channel_id=1, source_target_pairs={{0,15},{1,0},{2,1},{3,2},{4,3},{5,4},{6,5},{7,6},{8,7},{9,8},{10,9... | collective-permute-start | bytes 614408 | tf_op jit(solution)/shard_map/ppermute | solution.py:17
  54.1 5.6 %collective-permute-start.4 = (bf16[160,640]{1,0:T(8,128)(2,1)S(1)}, bf16[160,640]{1,0:T(8,128)(2,1)S(1)}, u32[]{:S(2)}, u32[]{:S(2)}) collective-permute-start(bf16[160,640]{1,0:T(8,128)(2,1)S(1)} %collective-permute-done.3), channel_id=1, source_target_pairs={{0,15},{1,0},{2,1},{3,2},{4,3},{5,4},{6,5},{7,6},{8,7},{9,8},{10,9... | collective-permute-start | bytes 614408 | tf_op jit(solution)/shard_map/ppermute | solution.py:17
  63.6 5.6 %collective-permute-start.5 = (bf16[160,640]{1,0:T(8,128)(2,1)S(1)}, bf16[160,640]{1,0:T(8,128)(2,1)S(1)}, u32[]{:S(2)}, u32[]{:S(2)}) collective-permute-start(bf16[160,640]{1,0:T(8,128)(2,1)S(1)} %collective-permute-done.4), channel_id=1, source_target_pairs={{0,15},{1,0},{2,1},{3,2},{4,3},{5,4},{6,5},{7,6},{8,7},{9,8},{10,9... | collective-permute-start | bytes 614408 | tf_op jit(solution)/shard_map/ppermute | solution.py:17
  73.2 5.6 %collective-permute-start.6 = (bf16[160,640]{1,0:T(8,128)(2,1)S(1)}, bf16[160,640]{1,0:T(8,128)(2,1)S(1)}, u32[]{:S(2)}, u32[]{:S(2)}) collective-permute-start(bf16[160,640]{1,0:T(8,128)(2,1)S(1)} %collective-permute-done.5), channel_id=1, source_target_pairs={{0,15},{1,0},{2,1},{3,2},{4,3},{5,4},{6,5},{7,6},{8,7},{9,8},{10,9... | collective-permute-start | bytes 614408 | tf_op jit(solution)/shard_map/ppermute | solution.py:17
  78.8 5.2 %collective-permute-done.6 = bf16[160,640]{1,0:T(8,128)(2,1)S(1)} collective-permute-done((bf16[160,640]{1,0:T(8,128)(2,1)S(1)}, bf16[160,640]{1,0:T(8,128)(2,1)S(1)}, u32[]{:S(2)}, u32[]{:S(2)}) %collective-permute-start.6) | collective-permute-done | bytes 204832 | tf_op jit(solution)/shard_map/ppermute | solution.py:17
  84.0 5.6 %collective-permute-start.7 = (bf16[160,640]{1,0:T(8,128)(2,1)S(1)}, bf16[160,640]{1,0:T(8,128)(2,1)}, u32[]{:S(2)}, u32[]{:S(2)}) collective-permute-start(bf16[160,640]{1,0:T(8,128)(2,1)S(1)} %collective-permute-done.6), channel_id=1, source_target_pairs={{0,15},{1,0},{2,1},{3,2},{4,3},{5,4},{6,5},{7,6},{8,7},{9,8},{10,9... | collective-permute-start | bytes 614408 | tf_op jit(solution)/shard_map/ppermute | solution.py:17
  94.5 5.7 %collective-permute-start.8 = (bf16[160,640]{1,0:T(8,128)(2,1)}, bf16[160,640]{1,0:T(8,128)(2,1)}, u32[]{:S(2)}, u32[]{:S(2)}) collective-permute-start(bf16[160,640]{1,0:T(8,128)(2,1)} %collective-permute-done.7), channel_id=1, source_target_pairs={{0,15},{1,0},{2,1},{3,2},{4,3},{5,4},{6,5},{7,6},{8,7},{9,8},{10,9... | collective-permute-start | bytes 614408 | tf_op jit(solution)/shard_map/ppermute | solution.py:17
  101.4 4.9 %collective-permute-done.8 = bf16[160,640]{1,0:T(8,128)(2,1)} collective-permute-done((bf16[160,640]{1,0:T(8,128)(2,1)}, bf16[160,640]{1,0:T(8,128)(2,1)}, u32[]{:S(2)}, u32[]{:S(2)}) %collective-permute-start.8) | collective-permute-done | bytes 204832 | tf_op jit(solution)/shard_map/ppermute | solution.py:17
  106.3 5.6 %collective-permute-start.9 = (bf16[160,640]{1,0:T(8,128)(2,1)}, bf16[160,640]{1,0:T(8,128)(2,1)}, u32[]{:S(2)}, u32[]{:S(2)}) collective-permute-start(bf16[160,640]{1,0:T(8,128)(2,1)} %collective-permute-done.8), channel_id=1, source_target_pairs={{0,15},{1,0},{2,1},{3,2},{4,3},{5,4},{6,5},{7,6},{8,7},{9,8},{10,9... | collective-permute-start | bytes 614408 | tf_op jit(solution)/shard_map/ppermute | solution.py:17
  127.9 5.5 %collective-permute-start.11 = (bf16[160,640]{1,0:T(8,128)(2,1)S(1)}, bf16[160,640]{1,0:T(8,128)(2,1)S(1)}, u32[]{:S(2)}, u32[]{:S(2)}) collective-permute-start(bf16[160,640]{1,0:T(8,128)(2,1)S(1)} %collective-permute-done.10), channel_id=1, source_target_pairs={{0,15},{1,0},{2,1},{3,2},{4,3},{5,4},{6,5},{7,6},{8,7},{9,8},{10,9... | collective-permute-start | bytes 614408 | tf_op jit(solution)/shard_map/ppermute | solution.py:17
  137.3 5.2 %collective-permute-start.12 = (bf16[160,640]{1,0:T(8,128)(2,1)S(1)}, bf16[160,640]{1,0:T(8,128)(2,1)S(1)}, u32[]{:S(2)}, u32[]{:S(2)}) collective-permute-start(bf16[160,640]{1,0:T(8,128)(2,1)S(1)} %collective-permute-done.11), channel_id=1, source_target_pairs={{0,15},{1,0},{2,1},{3,2},{4,3},{5,4},{6,5},{7,6},{8,7},{9,8},{10,9... | collective-permute-start | bytes 614408 | tf_op jit(solution)/shard_map/ppermute | solution.py:17
  146.0 5.6 %collective-permute-start.13 = (bf16[160,640]{1,0:T(8,128)(2,1)S(1)}, bf16[160,640]{1,0:T(8,128)(2,1)S(1)}, u32[]{:S(2)}, u32[]{:S(2)}) collective-permute-start(bf16[160,640]{1,0:T(8,128)(2,1)S(1)} %collective-permute-done.12), channel_id=1, source_target_pairs={{0,15},{1,0},{2,1},{3,2},{4,3},{5,4},{6,5},{7,6},{8,7},{9,8},{10,9... | collective-permute-start | bytes 614408 | tf_op jit(solution)/shard_map/ppermute | solution.py:17
  155.2 5.6 %collective-permute-start.14 = (bf16[160,640]{1,0:T(8,128)(2,1)S(1)}, bf16[160,640]{1,0:T(8,128)(2,1)S(1)}, u32[]{:S(2)}, u32[]{:S(2)}) collective-permute-start(bf16[160,640]{1,0:T(8,128)(2,1)S(1)} %collective-permute-done.13), channel_id=1, source_target_pairs={{0,15},{1,0},{2,1},{3,2},{4,3},{5,4},{6,5},{7,6},{8,7},{9,8},{10,9... | collective-permute-start | bytes 614408 | tf_op jit(solution)/shard_map/ppermute | solution.py:17
  161.2 3.7 %collective-permute-done.14 = bf16[160,640]{1,0:T(8,128)(2,1)S(1)} collective-permute-done((bf16[160,640]{1,0:T(8,128)(2,1)S(1)}, bf16[160,640]{1,0:T(8,128)(2,1)S(1)}, u32[]{:S(2)}, u32[]{:S(2)}) %collective-permute-start.14) | collective-permute-done | bytes 204832 | tf_op jit(solution)/shard_map/ppermute | solution.py:17
  166.7 8.8 %all-gather.7.cloned.1.call-done = bf16[1,2048,640]{1,2,0:T(8,128)(2,1)} async-done(((bf16[1,128,640]{1,2,0:T(8,128)(2,1)}), bf16[1,2048,640]{1,2,0:T(8,128)(2,1)}) %all-gather.7.cloned.1.call-update) | async-done | bytes 2621456 | tf_op jit(solution)/shard_map/all_gather | solution.py:62
  182.0 4.4 %copy.27 = bf16[2048,640]{1,0:T(8,128)(2,1)} copy(bf16[2048,640]{0,1:T(8,128)(2,1)} %bitcast.83) | data formatting | bytes 5242880 | tf_op jit(solution)/shard_map/convert_element_type | solution.py:75
  186.5 72.6 %reduce-scatter.5.cloned.1.call-done = bf16[128,640]{1,0:T(8,128)(2,1)} async-done(((bf16[2048,640]{1,0:T(8,128)(2,1)}), bf16[128,640]{1,0:T(8,128)(2,1)}) %reduce-scatter.5.cloned.1.call-update) | async-done | bytes 163856 | tf_op jit(solution)/shard_map/reduce_scatter | solution.py:74
  262.3 4.3 %copy.30 = bf16[2,128,2560]{1,0,2:T(2,128)(2,1)} copy(bf16[2,128,2560]{2,1,0:T(8,128)(2,1)} %convolution_convert_fusion) | data formatting | bytes 2621440
  269.2 27.2 %reduce-scatter.7.cloned.1.call-done = bf16[640,256]{1,0:T(8,128)(2,1)} async-done(((bf16[2560,256]{1,0:T(8,128)(2,1)}), bf16[640,256]{1,0:T(8,128)(2,1)}) %reduce-scatter.7.cloned.1.call-update) | async-done | bytes 327696
  304.8 12.7 %collective-permute-done.15 = bf16[2,128,640]{2,1,0:T(8,128)(2,1)} collective-permute-done((bf16[2,128,640]{2,1,0:T(8,128)(2,1)}, bf16[2,128,640]{2,1,0:T(8,128)(2,1)}, u32[]{:S(2)}, u32[]{:S(2)}) %collective-permute-start.15) | collective-permute-done | bytes 327712 | tf_op jit(solution)/shard_map/ppermute | solution.py:25
  (99 shorter events, 79.3 us)
Async XLA Ops:
  6.5 252.6 %copy-start = (bf16[1,2560,640]{2,1,0:T(8,128)(2,1)S(1)}, bf16[1,2560,640]{2,1,0:T(8,128)(2,1)}, u32[]{:S(2)}) copy-start(bf16[1,2560,640]{2,1,0:T(8,128)(2,1)} %param.13) | copy-start | bytes 9830404
  6.5 87.4 %copy-start.19 = (f32[1,2560]{1,0:T(1,128)S(1)}, f32[1,2560]{1,0:T(1,128)}, u32[]{:S(2)}) copy-start(f32[1,2560]{1,0:T(1,128)} %param.15) | copy-start | bytes 30724
  6.5 105.4 %all-gather.5.cloned.1.call-start = ((), (), s32[]{:S(2)}) async-start(), calls=%async_computation.3 | async-start | bytes 1638400 | tf_op jit(solution)/shard_map/all_gather | solution.py:45
  8.6 166.8 %all-gather.7.cloned.1.call-start = ((), (), s32[]{:S(2)}) async-start(), calls=%async_computation.4 | async-start | bytes 2785280 | tf_op jit(solution)/shard_map/all_gather | solution.py:62
  8.6 16.0 %collective-permute-start = (bf16[160,640]{1,0:T(8,128)(2,1)}, bf16[160,640]{1,0:T(8,128)(2,1)S(1)}, u32[]{:S(2)}, u32[]{:S(2)}) collective-permute-start(bf16[160,640]{1,0:T(8,128)(2,1)} %bitcast.90), channel_id=1, source_target_pairs={{0,15},{1,0},{2,1},{3,2},{4,3},{5,4},{6,5},{7,6},{8,7},{9,8},{10,9... | collective-permute-start | bytes 614408 | tf_op jit(solution)/shard_map/ppermute | solution.py:17
  25.4 8.9 %collective-permute-start.1 = (bf16[160,640]{1,0:T(8,128)(2,1)S(1)}, bf16[160,640]{1,0:T(8,128)(2,1)S(1)}, u32[]{:S(2)}, u32[]{:S(2)}) collective-permute-start(bf16[160,640]{1,0:T(8,128)(2,1)S(1)} %collective-permute-done), channel_id=1, source_target_pairs={{0,15},{1,0},{2,1},{3,2},{4,3},{5,4},{6,5},{7,6},{8,7},{9,8},{10,9... | collective-permute-start | bytes 614408 | tf_op jit(solution)/shard_map/ppermute | solution.py:17
  35.0 8.9 %collective-permute-start.2 = (bf16[160,640]{1,0:T(8,128)(2,1)S(1)}, bf16[160,640]{1,0:T(8,128)(2,1)S(1)}, u32[]{:S(2)}, u32[]{:S(2)}) collective-permute-start(bf16[160,640]{1,0:T(8,128)(2,1)S(1)} %collective-permute-done.1), channel_id=1, source_target_pairs={{0,15},{1,0},{2,1},{3,2},{4,3},{5,4},{6,5},{7,6},{8,7},{9,8},{10,9... | collective-permute-start | bytes 614408 | tf_op jit(solution)/shard_map/ppermute | solution.py:17
  44.5 8.9 %collective-permute-start.3 = (bf16[160,640]{1,0:T(8,128)(2,1)S(1)}, bf16[160,640]{1,0:T(8,128)(2,1)S(1)}, u32[]{:S(2)}, u32[]{:S(2)}) collective-permute-start(bf16[160,640]{1,0:T(8,128)(2,1)S(1)} %collective-permute-done.2), channel_id=1, source_target_pairs={{0,15},{1,0},{2,1},{3,2},{4,3},{5,4},{6,5},{7,6},{8,7},{9,8},{10,9... | collective-permute-start | bytes 614408 | tf_op jit(solution)/shard_map/ppermute | solution.py:17
  54.1 8.9 %collective-permute-start.4 = (bf16[160,640]{1,0:T(8,128)(2,1)S(1)}, bf16[160,640]{1,0:T(8,128)(2,1)S(1)}, u32[]{:S(2)}, u32[]{:S(2)}) collective-permute-start(bf16[160,640]{1,0:T(8,128)(2,1)S(1)} %collective-permute-done.3), channel_id=1, source_target_pairs={{0,15},{1,0},{2,1},{3,2},{4,3},{5,4},{6,5},{7,6},{8,7},{9,8},{10,9... | collective-permute-start | bytes 614408 | tf_op jit(solution)/shard_map/ppermute | solution.py:17
  63.6 9.0 %collective-permute-start.5 = (bf16[160,640]{1,0:T(8,128)(2,1)S(1)}, bf16[160,640]{1,0:T(8,128)(2,1)S(1)}, u32[]{:S(2)}, u32[]{:S(2)}) collective-permute-start(bf16[160,640]{1,0:T(8,128)(2,1)S(1)} %collective-permute-done.4), channel_id=1, source_target_pairs={{0,15},{1,0},{2,1},{3,2},{4,3},{5,4},{6,5},{7,6},{8,7},{9,8},{10,9... | collective-permute-start | bytes 614408 | tf_op jit(solution)/shard_map/ppermute | solution.py:17
  73.2 10.8 %collective-permute-start.6 = (bf16[160,640]{1,0:T(8,128)(2,1)S(1)}, bf16[160,640]{1,0:T(8,128)(2,1)S(1)}, u32[]{:S(2)}, u32[]{:S(2)}) collective-permute-start(bf16[160,640]{1,0:T(8,128)(2,1)S(1)} %collective-permute-done.5), channel_id=1, source_target_pairs={{0,15},{1,0},{2,1},{3,2},{4,3},{5,4},{6,5},{7,6},{8,7},{9,8},{10,9... | collective-permute-start | bytes 614408 | tf_op jit(solution)/shard_map/ppermute | solution.py:17
  84.0 10.5 %collective-permute-start.7 = (bf16[160,640]{1,0:T(8,128)(2,1)S(1)}, bf16[160,640]{1,0:T(8,128)(2,1)}, u32[]{:S(2)}, u32[]{:S(2)}) collective-permute-start(bf16[160,640]{1,0:T(8,128)(2,1)S(1)} %collective-permute-done.6), channel_id=1, source_target_pairs={{0,15},{1,0},{2,1},{3,2},{4,3},{5,4},{6,5},{7,6},{8,7},{9,8},{10,9... | collective-permute-start | bytes 614408 | tf_op jit(solution)/shard_map/ppermute | solution.py:17
  91.4 167.7 %reduce-scatter.5.cloned.1.call-start = ((), (), s32[]{:S(2)}) async-start(), calls=%async_computation.2 | async-start | bytes 2785280 | tf_op jit(solution)/shard_map/reduce_scatter | solution.py:74
  94.5 11.8 %collective-permute-start.8 = (bf16[160,640]{1,0:T(8,128)(2,1)}, bf16[160,640]{1,0:T(8,128)(2,1)}, u32[]{:S(2)}, u32[]{:S(2)}) collective-permute-start(bf16[160,640]{1,0:T(8,128)(2,1)} %collective-permute-done.7), channel_id=1, source_target_pairs={{0,15},{1,0},{2,1},{3,2},{4,3},{5,4},{6,5},{7,6},{8,7},{9,8},{10,9... | collective-permute-start | bytes 614408 | tf_op jit(solution)/shard_map/ppermute | solution.py:17
  106.3 13.4 %collective-permute-start.9 = (bf16[160,640]{1,0:T(8,128)(2,1)}, bf16[160,640]{1,0:T(8,128)(2,1)}, u32[]{:S(2)}, u32[]{:S(2)}) collective-permute-start(bf16[160,640]{1,0:T(8,128)(2,1)} %collective-permute-done.8), channel_id=1, source_target_pairs={{0,15},{1,0},{2,1},{3,2},{4,3},{5,4},{6,5},{7,6},{8,7},{9,8},{10,9... | collective-permute-start | bytes 614408 | tf_op jit(solution)/shard_map/ppermute | solution.py:17
  119.8 8.1 %collective-permute-start.10 = (bf16[160,640]{1,0:T(8,128)(2,1)}, bf16[160,640]{1,0:T(8,128)(2,1)S(1)}, u32[]{:S(2)}, u32[]{:S(2)}) collective-permute-start(bf16[160,640]{1,0:T(8,128)(2,1)} %collective-permute-done.9), channel_id=1, source_target_pairs={{0,15},{1,0},{2,1},{3,2},{4,3},{5,4},{6,5},{7,6},{8,7},{9,8},{10,9... | collective-permute-start | bytes 614408 | tf_op jit(solution)/shard_map/ppermute | solution.py:17
  127.9 9.4 %collective-permute-start.11 = (bf16[160,640]{1,0:T(8,128)(2,1)S(1)}, bf16[160,640]{1,0:T(8,128)(2,1)S(1)}, u32[]{:S(2)}, u32[]{:S(2)}) collective-permute-start(bf16[160,640]{1,0:T(8,128)(2,1)S(1)} %collective-permute-done.10), channel_id=1, source_target_pairs={{0,15},{1,0},{2,1},{3,2},{4,3},{5,4},{6,5},{7,6},{8,7},{9,8},{10,9... | collective-permute-start | bytes 614408 | tf_op jit(solution)/shard_map/ppermute | solution.py:17
  137.3 8.7 %collective-permute-start.12 = (bf16[160,640]{1,0:T(8,128)(2,1)S(1)}, bf16[160,640]{1,0:T(8,128)(2,1)S(1)}, u32[]{:S(2)}, u32[]{:S(2)}) collective-permute-start(bf16[160,640]{1,0:T(8,128)(2,1)S(1)} %collective-permute-done.11), channel_id=1, source_target_pairs={{0,15},{1,0},{2,1},{3,2},{4,3},{5,4},{6,5},{7,6},{8,7},{9,8},{10,9... | collective-permute-start | bytes 614408 | tf_op jit(solution)/shard_map/ppermute | solution.py:17
  146.0 9.3 %collective-permute-start.13 = (bf16[160,640]{1,0:T(8,128)(2,1)S(1)}, bf16[160,640]{1,0:T(8,128)(2,1)S(1)}, u32[]{:S(2)}, u32[]{:S(2)}) collective-permute-start(bf16[160,640]{1,0:T(8,128)(2,1)S(1)} %collective-permute-done.12), channel_id=1, source_target_pairs={{0,15},{1,0},{2,1},{3,2},{4,3},{5,4},{6,5},{7,6},{8,7},{9,8},{10,9... | collective-permute-start | bytes 614408 | tf_op jit(solution)/shard_map/ppermute | solution.py:17
  155.2 9.6 %collective-permute-start.14 = (bf16[160,640]{1,0:T(8,128)(2,1)S(1)}, bf16[160,640]{1,0:T(8,128)(2,1)S(1)}, u32[]{:S(2)}, u32[]{:S(2)}) collective-permute-start(bf16[160,640]{1,0:T(8,128)(2,1)S(1)} %collective-permute-done.13), channel_id=1, source_target_pairs={{0,15},{1,0},{2,1},{3,2},{4,3},{5,4},{6,5},{7,6},{8,7},{9,8},{10,9... | collective-permute-start | bytes 614408 | tf_op jit(solution)/shard_map/ppermute | solution.py:17
  186.4 72.7 %copy-start.17 = (bf16[1,128,640]{2,1,0:T(8,128)(2,1)S(1)}, bf16[1,128,640]{2,1,0:T(8,128)(2,1)}, u32[]{:S(2)}) copy-start(bf16[1,128,640]{2,1,0:T(8,128)(2,1)} %get-tuple-element.6) | copy-start | bytes 491524
  186.4 110.0 %reduce-scatter.7.cloned.1.call-start = ((), (), s32[]{:S(2)}) async-start(), calls=%async_computation.5 | async-start | bytes 1638400
  269.2 35.5 %copy-start.18 = (bf16[128,640]{1,0:T(8,128)(2,1)S(1)}, bf16[128,640]{1,0:T(8,128)(2,1)}, u32[]{:S(2)}) copy-start(bf16[128,640]{1,0:T(8,128)(2,1)} %param.10) | copy-start | bytes 491524
  302.0 15.5 %collective-permute-start.15 = (bf16[2,128,640]{2,1,0:T(8,128)(2,1)}, bf16[2,128,640]{2,1,0:T(8,128)(2,1)}, u32[]{:S(2)}, u32[]{:S(2)}) collective-permute-start(bf16[2,128,640]{2,1,0:T(8,128)(2,1)} %fusion.5), channel_id=1, source_target_pairs={{64,0},{128,64},{192,128},{256,192},{320,256},{384,320},{448,384},... | collective-permute-start | bytes 983048 | tf_op jit(solution)/shard_map/ppermute | solution.py:25
  (16 other events, 42.6 us)
Sparse Core Ops, SparseCore 0:
  9.5 34.6 all-gather.4
  91.5 83.8 all-gather.6
  186.5 72.4 reduce-scatter.4
  269.3 27.0 reduce-scatter.6
